TPU v7x, 32 devices: a whole 2x2x4 slice. The times are simulated.
32 devices in a mesh: row: 8 (over z, y), col: 4 (over x, core).
Axes of the slice: x: 2, y: 2, z: 4, core: 2. Of those that a mesh axis runs over, the one named last changes fastest.
Arguments:
- pair_rep: bfloat16 [1024, 1024, 128], P('row', 'col'), may hold values from -8 to 8
- row_ids: int32 [16], P('row'), may hold values from 0 to 1023, as said below
- pad_mask: int32 [1024], P('col'), may hold values from 0 to 1, as said below
- ln_gain: float32 [128], replicated, may hold values from 0.25 to 1.75
- ln_bias: float32 [128], replicated, may hold values from -2 to 2
- w_query: bfloat16 [128, 128], replicated, may hold values from -2 to 2
- w_key: bfloat16 [128, 128], replicated, may hold values from -2 to 2
- w_value: bfloat16 [128, 128], replicated, may hold values from -0.5 to 0.5
- w_gate: bfloat16 [128, 128], replicated, may hold values from -0.5 to 0.5
- gate_bias: float32 [128], replicated, may hold values from -4 to 4
- w_bias: bfloat16 [128, 4], replicated, may hold values from -0.5 to 0.5
- w_out: bfloat16 [128, 128], replicated, may hold values from -0.5 to 0.5
Outputs:
- update: bfloat16 [16, 1024, 128], P('col', 'row')
Inputs may be any that keep to these rules, and one draw needn't show every extreme that they name: `row_ids`: entries t * 2 to t * 2 + 1 are distinct and lie in [t * 128, (t + 1) * 128). `pad_mask`: A prefix of the tokens is real and the rest is padding; the first 257 tokens are real.
All inputs are finite; a program needn't handle non-finite values.
Results may differ from a plain program's by a relative error of at most 0.023.
Values may be sent and summed in bfloat16 or wider, within the bound.
A program may use at most 128 MiB of HBM per device.

v0:
```python
import jax
import jax.numpy as jnp
from jax import lax
from jax.sharding import PartitionSpec as P


def from_root(value, axis, source):
    kept = jnp.where(lax.axis_index(axis) == source, value, 0).astype(value.dtype)
    return lax.psum(kept, axis)


def merged(value, axis, join):
    gathered = jax.tree.map(
        lambda a, kind: lax.all_gather(a.astype(kind), axis),
        value,
        (jnp.bfloat16, jnp.bfloat16, jnp.bfloat16),
    )

    def take(source):
        return jax.tree.map(
            lambda a, own: lax.dynamic_index_in_dim(a, source, 0, False).astype(own.dtype),
            gathered,
            value,
        )

    return lax.fori_loop(
        1, lax.axis_size(axis), lambda source, state: join(state, take(source)), take(0)
    )


def layer_norm(values, ln_gain, ln_bias):
    values = values.astype(jnp.float32)
    centre = jnp.mean(values, axis=-1, keepdims=True)
    spread = jnp.mean((values - centre) ** 2, axis=-1, keepdims=True)
    return ((values - centre) * lax.rsqrt(spread + 1e-05) * ln_gain + ln_bias).astype(jnp.bfloat16)


def project(normed, weight):
    flat = normed.reshape(-1, normed.shape[-1])
    return jnp.dot(flat, weight, preferred_element_type=jnp.float32).reshape(
        normed.shape[:-1] + (weight.shape[1],)
    )


def query_gate(normed, w_query, w_gate, gate_bias, head_dim):
    query = (project(normed, w_query) / jnp.sqrt(jnp.float32(head_dim))).astype(jnp.bfloat16)
    gate = jax.nn.sigmoid(project(normed, w_gate) + gate_bias).astype(jnp.bfloat16)
    return jnp.concatenate([query, gate], axis=-1)


def key_value(normed, w_key, w_value):
    return jnp.concatenate(
        [
            project(normed, w_key).astype(jnp.bfloat16),
            project(normed, w_value).astype(jnp.bfloat16),
        ],
        axis=-1,
    )


def combine_parts(first, second):
    peak_a, total_a, summed_a = first
    peak_b, total_b, summed_b = second
    peak = jnp.maximum(peak_a, peak_b)
    scale_a = jnp.exp(peak_a - peak)
    scale_b = jnp.exp(peak_b - peak)
    return (
        peak,
        total_a * scale_a + total_b * scale_b,
        summed_a * scale_a[..., None] + summed_b * scale_b[..., None],
    )


def body(
    pair_rep,
    row_ids,
    pad_mask,
    ln_gain,
    ln_bias,
    w_query,
    w_key,
    w_value,
    w_gate,
    gate_bias,
    w_bias,
    w_out,
):
    rows_here = pair_rep.shape[0]
    cols_here = pair_rep.shape[1]
    heads = w_bias.shape[1]
    width = w_query.shape[1]
    head_dim = width // heads
    n_col = lax.axis_size("col")
    row_index = lax.axis_index("row")
    col_index = lax.axis_index("col")
    normed = layer_norm(pair_rep, ln_gain, ln_bias)
    offsets = row_ids - row_index * rows_here
    slice_start = row_index * rows_here % cols_here
    root_col = row_index * rows_here // cols_here
    raw_chosen = jnp.take(pair_rep, offsets, axis=0)
    raw_all = lax.all_gather(raw_chosen, "row", axis=0, tiled=True)
    keys_values = key_value(layer_norm(raw_all, ln_gain, ln_bias), w_key, w_value)
    raw_mine = lax.dynamic_slice_in_dim(raw_all, slice_start, rows_here, 1)
    raw_mine = from_root(raw_mine, "col", root_col)
    query_gates = query_gate(
        layer_norm(raw_mine, ln_gain, ln_bias), w_query, w_gate, gate_bias, head_dim
    )
    selected = query_gates.shape[0]
    pair_bias = jnp.einsum("jkc,ch->hjk", normed, w_bias, preferred_element_type=jnp.float32)
    key_live = pad_mask > 0
    query = query_gates[..., :width].reshape(4, selected // 4, rows_here, heads, head_dim)
    gate = query_gates[..., width:]
    key_rows = keys_values[..., :width].reshape(4, selected // 4, cols_here, heads, head_dim)
    value_rows = keys_values[..., width:].reshape(4, selected // 4, cols_here, heads, head_dim)

    def partial_block(items):
        query_block, key_block, value_block = items
        scores = jnp.einsum(
            "tjhd,tkhd->thjk", query_block, key_block, preferred_element_type=jnp.float32
        )
        scores = scores + pair_bias[None]
        scores = jnp.where(key_live[None, None, None, :], scores, jnp.float32(-1000000000.0))
        peak = jnp.max(scores, axis=-1)
        expo = jnp.exp(scores - peak[..., None])
        totals = jnp.sum(expo, axis=-1)
        summed = jnp.einsum(
            "thjk,tkhd->thjd",
            expo.astype(jnp.bfloat16),
            value_block,
            preferred_element_type=jnp.float32,
        )
        return (peak, totals, summed)

    peak, totals, summed = lax.map(partial_block, (query, key_rows, value_rows))
    peak = peak.reshape(selected, heads, rows_here)
    totals = totals.reshape(selected, heads, rows_here)
    summed = summed.reshape(selected, heads, rows_here, head_dim)
    row_count = selected // n_col
    peak, totals, summed = merged((peak, totals, summed), "col", combine_parts)
    totals = lax.dynamic_slice_in_dim(totals, col_index * row_count, row_count, 0)
    summed = lax.dynamic_slice_in_dim(summed, col_index * row_count, row_count, 0)
    attended = summed / totals[..., None]
    attended = jnp.transpose(attended, (0, 2, 1, 3)).reshape(row_count, rows_here, width)
    gate_mine = lax.dynamic_slice_in_dim(gate, col_index * row_count, row_count, 0)
    gated = (gate_mine.astype(jnp.float32) * attended).astype(jnp.bfloat16)
    return project(gated, w_out).astype(jnp.bfloat16)


def solution(mesh):
    return jax.shard_map(
        body,
        mesh=mesh,
        in_specs=(
            P("row", "col", None),
            P("row"),
            P("col"),
            P(),
            P(),
            P(),
            P(),
            P(),
            P(),
            P(),
            P(),
            P(),
        ),
        out_specs=P("col", "row", None),
        check_vma=False,
    )
```

profile of v0, /device:TPU:0, one launch (start us, length us, event | category | flops | bytes accessed | tf_op | source)
XLA Modules:
  0.0 170.1 jit_solution(14934871690667444920)
XLA Ops:
  6.5 0.7 compare_and_fusion
  7.2 4.0 %gather_fusion = bf16[2,256,128]{2,1,0:T(8,128)(2,1)S(1)} fusion(bf16[128,256,128]{2,1,0:T(8,128)(2,1)} %param.16, s32[1024]{0:T(1024)S(1)} %pad_clamp_fusion), kind=kCustom, calls=%fused_computation | custom fusion | bytes 262152 | tf_op jit(solution)/shard_map/jit(_take)/gather | solution.py:100
  11.2 0.7 broadcast_select_fusion
  11.9 0.0 all-gather.3.cloned.1.call-update
  11.9 0.0 all-reduce.2.cloned.1.call-start
  12.0 5.7 %convert_reduce_fusion = f32[128,256]{1,0:T(8,128)S(1)} fusion(bf16[128,256,128]{2,1,0:T(8,128)(2,1)} %param.16), kind=kLoop, calls=%fused_computation.37 | loop fusion | flops 8355840 | bytes 8519680 | tf_op jit(solution)/shard_map/reduce_sum | solution.py:33
  17.7 0.0 copy-start.5
  17.7 0.0 copy-start.6
  17.8 0.0 copy-start.10
  17.8 10.7 %fusion.23 = f32[128,256]{1,0:T(8,128)S(1)} fusion(bf16[128,256,128]{2,1,0:T(8,128)(2,1)} %param.16, f32[128,256]{1,0:T(8,128)S(1)} %broadcast_multiply_fusion), kind=kLoop, calls=%fused_computation.40 | loop fusion | flops 16744448 | bytes 8650752 | tf_op jit(solution)/shard_map/reduce_sum | solution.py:34
  28.6 11.4 %fusion.38 = f32[4,128,256]{2,0,1:T(4,128)S(1)} fusion(bf16[128,256,128]{2,1,0:T(8,128)(2,1)} %param.16, f32[128]{0:T(128)S(1)} %copy-done.5, f32[128]{0:T(128)S(1)} %copy-done.6, f32[128,256]{1,0:T(8,128)S(1)} %add_rsqrt_fusion, f32[128,256]{1,0:T(8,128)S(1)} %broadcast_multiply_fusion, bf16[128,4]{0,1:T(4,128)(2,1)S(1)} %copy-done.10), kind=kOutput, calls=%fused_computation.61 | convolution fusion | flops 58720256 | bytes 9177088 | tf_op jit(solution)/shard_map/jkc,ch->hjk/dot_general | solution.py:109
  39.9 0.1 copy.28
  40.1 15.1 %all-gather.3.cloned.1.call-done = bf16[16,256,128]{2,1,0:T(8,128)(2,1)} async-done(((bf16[2,256,128]{2,1,0:T(8,128)(2,1)}), bf16[16,256,128]{2,1,0:T(8,128)(2,1)}) %all-gather.3.cloned.1.call-update) | async-done | bytes 1048592 | tf_op jit(solution)/shard_map/all_gather | solution.py:101
  55.2 2.1 %dynamic-slice_select_fusion = bf16[16,128,128]{2,1,0:T(8,128)(2,1)} fusion(bf16[16,256,128]{2,1,0:T(8,128)(2,1)} %all-gather.3.cloned.1.call-done, s32[]{:T(128)S(6)} %select_n.62, pred[]{:T(512)S(6)} %eq.5), kind=kLoop, calls=%fused_computation.69 | loop fusion | flops 262144 | bytes 1048581 | tf_op jit(solution)/shard_map/jit(_where)/select_n | solution.py:8
  57.2 0.0 all-reduce.2.cloned.1.call-update
  57.3 0.0 all-gather.5.cloned.1.call-start
  57.3 0.3 convert_reduce_fusion.1
  57.7 0.0 copy-start.7
  57.7 1.3 fusion.31
  59.0 1.7 convolution_convert_fusion.1
  60.7 0.0 copy-start.8
  60.7 2.5 %convolution_convert_fusion = bf16[16,256,128]{1,2,0:T(8,128)(2,1)} fusion(bf16[16,256,128]{2,1,0:T(8,128)(2,1)S(1)} %copy-done.1, f32[128]{0:T(128)S(1)} %copy-done.5, f32[128]{0:T(128)S(1)} %copy-done.6, f32[16,256]{1,0:T(8,128)S(1)} %add_rsqrt_fusion.1, f32[16,256]{1,0:T(8,128)S(1)} %broadcast_multiply_fusion.1, bf16[128,128]{1,0:T(8,128)(2,1)S(1)} %copy-done.7), kind=kOutput, calls=%fused_computation.53 | convolution fusion | flops 137887744 | bytes 2163712 | tf_op jit(solution)/shard_map/dot_general | solution.py:40
  63.2 26.5 %all-reduce.2.cloned.1.call-done = bf16[16,128,128]{2,1,0:T(8,128)(2,1)} async-done(((bf16[16,128,128]{2,1,0:T(8,128)(2,1)}), bf16[16,128,128]{2,1,0:T(8,128)(2,1)}) %all-reduce.2.cloned.1.call-update) | async-done | bytes 524304 | tf_op jit(solution)/shard_map/psum | solution.py:9
  89.7 1.2 convert_reduce_fusion.2
  91.0 1.7 fusion.41
  92.7 1.9 %fusion.35 = bf16[16,128,128]{1,2,0:T(8,128)(2,1)S(1)} fusion(bf16[16,128,128]{2,1,0:T(8,128)(2,1)} %all-reduce.2.cloned.1.call-done, f32[128]{0:T(128)S(1)} %copy-done.5, f32[128]{0:T(128)S(1)} %copy-done.6, f32[16,128]{1,0:T(8,128)S(1)} %add_rsqrt_fusion.2, f32[16,128]{1,0:T(8,128)S(1)} %broadcast_multiply_fusion.2, bf16[128,128]{1,0:T(8,128)(2,1)S(1)} %copy-done.8), kind=kOutput, calls=%fused_computation.58 | convolution fusion | flops 69206016 | bytes 1098752 | tf_op jit(solution)/shard_map/dot_general | solution.py:40
  94.6 0.0 copy-start.4
  94.6 12.7 %while.33 = (s32[]{:T(128)}, bf16[4,4,4,128]{3,2,1,0:T(4,128)(2,1)S(1)}, bf16[4,4,4,128]{3,2,1,0:T(4,128)(2,1)S(1)}, bf16[4,4,4,128,32]{3,4,2,1,0:T(8,128)(2,1)S...) while((s32[]{:T(128)}, ...), condition=%wide.region_10.11_spmd, body=%wide.region_7.10_spmd.sunk | while | flops 72871936 | bytes 8838517 | solution.py:134
  94.6 0.6 fusion.76
  95.2 0.9 fusion.77
  96.1 1.6 fusion.78
  97.8 0.6 fusion.76
  98.4 0.9 fusion.77
  99.3 1.6 fusion.78
  100.9 0.6 fusion.76
  101.5 0.9 fusion.77
  102.5 1.6 fusion.78
  104.1 0.6 fusion.76
  104.7 0.9 fusion.77
  105.6 1.6 fusion.78
  107.3 0.8 copy-done.3
  108.1 0.0 all-gather.5.cloned.1.call-update
  108.1 5.2 %all_gather.16 = bf16[4,16,4,128]{3,1,2,0:T(8,128)(2,1)S(1)} all-gather(bf16[1,16,4,128]{3,1,2,0:T(8,128)(2,1)S(1)} %bitcast.102), channel_id=1, replica_groups=mesh['row'=8,'col'=4] {'col'}, dimensions={0}, use_global_device_ids=true | all-gather | bytes 81920 | tf_op jit(solution)/shard_map/all_gather | solution.py:14
  113.4 5.4 %all_gather.17 = bf16[4,16,4,128]{3,1,2,0:T(8,128)(2,1)S(1)} all-gather(bf16[1,16,4,128]{3,1,2,0:T(8,128)(2,1)S(1)} %bitcast.103), channel_id=1, replica_groups=mesh['row'=8,'col'=4] {'col'}, dimensions={0}, use_global_device_ids=true | all-gather | bytes 81920 | tf_op jit(solution)/shard_map/all_gather | solution.py:14
  118.9 1.7 %fusion.49 = f32[16,128,128]{2,1,0:T(8,128)} fusion(bf16[16,128,128]{2,1,0:T(8,128)(2,1)S(1)} %copy-done.2, f32[128]{0:T(128)S(1)} %copy-done.5, f32[128]{0:T(128)S(1)} %copy-done.6, f32[16,128]{1,0:T(8,128)S(1)} %add_rsqrt_fusion.2, f32[16,128]{1,0:T(8,128)S(1)} %broadcast_multiply_fusion.2, bf16[128,128]{1,0:T(8,128)(2,1)S(1)} %copy-done.4), kind=kOutput, calls=%fused_computation.70 | convolution fusion | flops 68681728 | bytes 1623040 | tf_op jit(solution)/shard_map/dot_general | solution.py:40
  120.6 10.3 %all-gather.5.cloned.1.call-done = bf16[4,16,4,128,32]{3,4,2,1,0:T(8,128)(2,1)} async-done(((bf16[1,16,4,128,32]{3,4,2,1,0:T(8,128)(2,1)}), bf16[4,16,4,128,32]{3,4,2,1,0:T(8,128)(2,1)}) %all-gather.5.cloned.1.call-update) | async-done | bytes 2097168 | tf_op jit(solution)/shard_map/all_gather | solution.py:14
  130.9 1.2 fusion.47
  132.1 2.6 %copy.33 = f32[16,4,128,32]{3,2,1,0:T(8,128)} copy(f32[16,4,128,32]{2,3,1,0:T(8,128)S(1)} %fusion.47) | data formatting | bytes 2097152 | tf_op jit(solution)/shard_map/while | solution.py:26
  134.7 24.0 %while.34 = (s32[]{:T(128)}, f32[16,4,128]{2,1,0:T(4,128)S(1)}, f32[16,4,128]{2,1,0:T(4,128)S(1)}, f32[16,4,128,32]{3,2,1,0:T(8,128)}, bf16[4,16,4,128]{3,1,2,0:...) while((s32[]{:T(128)}, f32[16,4,128]{2,1,0:T(4,128)S(1)}, ...), condition=%wide.region_12.13_spmd, body=%wide.region_11.12_spmd.sunk | while | flops 1114117 | bytes 5079191 | solution.py:26
  134.8 0.1 fusion.79
  134.8 1.1 constant_dynamic-slice_fusion.7
  135.9 1.0 copy.61
  136.9 5.8 %fusion.80 = f32[16,4,128,32]{3,2,1,0:T(8,128)} fusion(f32[16,4,128,32]{3,2,1,0:T(8,128)} %get-tuple-element.469, bf16[1,16,4,128,32]{4,3,2,1,0:T(8,128)(2,1)S(1)} %copy.61, f32[16,4,128]{2,1,0:T(4,128)S(1)} %get-tuple-element.424, f32[16,4,128]{2,1,0:T(4,128)S(1)} %get-tuple-element.425), kind=kLoop, calls=%fused_computation.24.clone.1 | loop fusion | flops 1048576 | bytes 2686976 | tf_op jit(solution)/shard_map/while/body/eval_jaxpr/add | solution.py:70
  142.8 0.1 fusion.79
  142.8 1.1 constant_dynamic-slice_fusion.7
  143.9 1.0 copy.61
  145.0 5.8 %fusion.80 = f32[16,4,128,32]{3,2,1,0:T(8,128)} fusion(f32[16,4,128,32]{3,2,1,0:T(8,128)} %get-tuple-element.469, bf16[1,16,4,128,32]{4,3,2,1,0:T(8,128)(2,1)S(1)} %copy.61, f32[16,4,128]{2,1,0:T(4,128)S(1)} %get-tuple-element.424, f32[16,4,128]{2,1,0:T(4,128)S(1)} %get-tuple-element.425), kind=kLoop, calls=%fused_computation.24.clone.1 | loop fusion | flops 1048576 | bytes 2686976 | tf_op jit(solution)/shard_map/while/body/eval_jaxpr/add | solution.py:70
  150.8 0.1 fusion.79
  150.8 1.1 constant_dynamic-slice_fusion.7
  151.9 1.0 copy.61
  153.0 5.8 %fusion.80 = f32[16,4,128,32]{3,2,1,0:T(8,128)} fusion(f32[16,4,128,32]{3,2,1,0:T(8,128)} %get-tuple-element.469, bf16[1,16,4,128,32]{4,3,2,1,0:T(8,128)(2,1)S(1)} %copy.61, f32[16,4,128]{2,1,0:T(4,128)S(1)} %get-tuple-element.424, f32[16,4,128]{2,1,0:T(4,128)S(1)} %get-tuple-element.425), kind=kLoop, calls=%fused_computation.24.clone.1 | loop fusion | flops 1048576 | bytes 2686976 | tf_op jit(solution)/shard_map/while/body/eval_jaxpr/add | solution.py:70
  158.8 2.8 %copy.37 = f32[16,4,128,32]{2,3,1,0:T(8,128)S(1)} copy(f32[16,4,128,32]{3,2,1,0:T(8,128)} %get-tuple-element.234) | data formatting | bytes 2097152 | tf_op jit(solution)/shard_map/while | solution.py:26
  161.6 0.1 copy.38
  161.8 1.8 %convolution_convert_fusion.2 = bf16[4,128,128]{2,1,0:T(8,128)(2,1)} fusion(f32[4,128,128]{2,1,0:T(8,128)S(1)} %copy.38, f32[16,128,128]{2,1,0:T(8,128)} %fusion.49, s32[]{:T(128)S(6)} %select_n.64, f32[128]{0:T(128)S(1)} %copy-done.12, bf16[128,128]{1,0:T(8,128)(2,1)S(1)} %copy-done.9), kind=kOutput, calls=%fused_computation.62 | convolution fusion | flops 17367040 | bytes 688644 | tf_op jit(solution)/shard_map/dot_general | solution.py:40
  (50 shorter events, 0.3 us)
Async XLA Ops:
  6.5 52.5 %copy-start = (bf16[128,128]{1,0:T(8,128)(2,1)S(1)}, bf16[128,128]{1,0:T(8,128)(2,1)}, u32[]{:S(2)}) copy-start(bf16[128,128]{1,0:T(8,128)(2,1)} %param.22) | copy-start | bytes 98308
  6.5 48.6 %all-gather.3.cloned.1.call-start = ((), (), s32[]{:S(2)}) async-start(), calls=%async_computation | async-start | bytes 1179648 | tf_op jit(solution)/shard_map/all_gather | solution.py:101
  11.9 77.8 %all-reduce.2.cloned.1.call-start = ((), (), s32[]{:S(2)}) async-start(), calls=%async_computation.1 | async-start | bytes 1048576 | tf_op jit(solution)/shard_map/psum | solution.py:9
  17.7 10.8 %copy-start.5 = (f32[128]{0:T(128)S(1)}, f32[128]{0:T(128)}, u32[]{:S(2)}) copy-start(f32[128]{0:T(128)} %param.20) | copy-start | bytes 1540
  17.7 10.8 %copy-start.6 = (f32[128]{0:T(128)S(1)}, f32[128]{0:T(128)}, u32[]{:S(2)}) copy-start(f32[128]{0:T(128)} %param.19) | copy-start | bytes 1540
  17.8 10.8 %copy-start.10 = (bf16[128,4]{0,1:T(4,128)(2,1)S(1)}, bf16[128,4]{0,1:T(4,128)(2,1)}, u32[]{:S(2)}) copy-start(bf16[128,4]{0,1:T(4,128)(2,1)} %param.26) | copy-start | bytes 3076
  28.6 11.5 %copy-start.11 = (s32[256]{0:T(256)S(1)}, s32[256]{0:T(256)}, u32[]{:S(2)}) copy-start(s32[256]{0:T(256)} %param.18) | copy-start | bytes 3076
  55.2 2.1 %copy-start.1 = (bf16[16,256,128]{2,1,0:T(8,128)(2,1)S(1)}, bf16[16,256,128]{2,1,0:T(8,128)(2,1)}, u32[]{:S(2)}) copy-start(bf16[16,256,128]{2,1,0:T(8,128)(2,1)} %all-gather.3.cloned.1.call-done) | copy-start | bytes 3145732
  57.3 73.7 %all-gather.5.cloned.1.call-start = ((), (), s32[]{:S(2)}) async-start(), calls=%async_computation.2 | async-start | bytes 2621440 | tf_op jit(solution)/shard_map/all_gather | solution.py:14
  57.7 3.0 %copy-start.7 = (bf16[128,128]{1,0:T(8,128)(2,1)S(1)}, bf16[128,128]{1,0:T(8,128)(2,1)}, u32[]{:S(2)}) copy-start(bf16[128,128]{1,0:T(8,128)(2,1)} %param.23) | copy-start | bytes 98308
  60.7 31.9 %copy-start.8 = (bf16[128,128]{1,0:T(8,128)(2,1)S(1)}, bf16[128,128]{1,0:T(8,128)(2,1)}, u32[]{:S(2)}) copy-start(bf16[128,128]{1,0:T(8,128)(2,1)} %param.21) | copy-start | bytes 98308
  94.5 24.3 %copy-start.2 = (bf16[16,128,128]{2,1,0:T(8,128)(2,1)S(1)}, bf16[16,128,128]{2,1,0:T(8,128)(2,1)}, u32[]{:S(2)}) copy-start(bf16[16,128,128]{2,1,0:T(8,128)(2,1)} %all-reduce.2.cloned.1.call-done) | copy-start | bytes 1572868
  94.6 24.3 %copy-start.4 = (bf16[128,128]{1,0:T(8,128)(2,1)S(1)}, bf16[128,128]{1,0:T(8,128)(2,1)}, u32[]{:S(2)}) copy-start(bf16[128,128]{1,0:T(8,128)(2,1)} %param.24) | copy-start | bytes 98308
  107.3 0.8 copy-start.3
  158.8 3.0 %copy-start.9 = (bf16[128,128]{1,0:T(8,128)(2,1)S(1)}, bf16[128,128]{1,0:T(8,128)(2,1)}, u32[]{:S(2)}) copy-start(bf16[128,128]{1,0:T(8,128)(2,1)} %param.27) | copy-start | bytes 98308
  158.8 3.0 %copy-start.12 = (f32[128]{0:T(128)S(1)}, f32[128]{0:T(128)}, u32[]{:S(2)}) copy-start(f32[128]{0:T(128)} %param.25) | copy-start | bytes 1540
Sparse Core Ops, SparseCore 0:
  12.1 43.0 all-gather.2
  57.5 32.1 all-reduce.1
  108.2 22.6 all-gather.4
where the time goes:
time: 171 us; the launch traced here: 170 us
  waiting for transfers between devices  52 us (30%)
  other arithmetic  46.9 us (27%)
  matrix products  29.8 us (17%)
  local copies, waits for them, and re-layouts  17 us (10%)
  between operations  13.5 us (8%)
  blocking collectives  10.7 us (6%)
    psum x1, waiting for transfers between devices, from_root(): return lax.psum(kept, axis)  26.5 us
    add x3, other arithmetic, combine_parts(): summed_a * scale_a[..., None] + summed_b * scale_b[..., None]  17.4 us
    all_gather x1, waiting for transfers between devices, body(): raw_all = lax.all_gather(raw_chosen, 'row', axis=0, tiled=True)  15.1 us
    reduce_sum x3, other arithmetic, layer_norm(): spread = jnp.mean((values - centre) ** 2, axis=-1, keepdims=True)  13.7 us
    dot_general x1, matrix products, body(): jnp.einsum('jkc,ch->hjk', normed, w_bias, preferred_element_type=jnp.floa...  11.4 us
    all_gather x2, blocking collectives, merged(): lax.all_gather(a.astype(kind), axis)  10.7 us
    all_gather x1, waiting for transfers between devices, merged(): lax.all_gather(a.astype(kind), axis)  10.3 us
    dot_general x5, matrix products, project(): jnp.dot(flat, weight, preferred_element_type=jnp.float32)  9.55 us
  transfers between devices with their start and end apart: 3, of which 3 were waited for; matrix products, arithmetic and copies ran while one was open for 21% of the time, Pallas kernels for 0%

commit v1 on v0

v1 whole, which is shorter than its diff:
```python
import functools
import jax
import jax.numpy as jnp
from jax import lax
from jax.experimental import pallas as pl
from jax.experimental.pallas import tpu as pltpu
from jax.sharding import PartitionSpec as P

F32 = jnp.float32
BF16 = jnp.bfloat16
VM = pl.BlockSpec(memory_space=pltpu.VMEM)
ROWS_CHUNK = 16
ROWS_STEP = 8


def norm_kernel(ids, x_ref, gain_ref, shift_ref, o_ref):
    x = x_ref[0].astype(F32)
    centre = jnp.mean(x, axis=-1, keepdims=True)
    d = x - centre
    spread = jnp.mean(d * d, axis=-1, keepdims=True)
    o_ref[0] = (d * lax.rsqrt(spread + 1e-05) * gain_ref[...] + shift_ref[...]).astype(BF16)


def chosen_normed(pair_rep, offsets, gain, shift):
    rows, cols, cz = pair_rep.shape
    return pl.pallas_call(
        norm_kernel,
        out_shape=jax.ShapeDtypeStruct((offsets.shape[0], cols, cz), BF16),
        grid_spec=pltpu.PrefetchScalarGridSpec(
            num_scalar_prefetch=1,
            grid=(offsets.shape[0],),
            in_specs=[
                pl.BlockSpec((1, cols, cz), lambda i, ids: (ids[i], 0, 0)),
                pl.BlockSpec((1, cz), lambda i, ids: (0, 0)),
                pl.BlockSpec((1, cz), lambda i, ids: (0, 0)),
            ],
            out_specs=pl.BlockSpec((1, cols, cz), lambda i, ids: (i, 0, 0)),
        ),
    )(offsets, pair_rep, gain, shift)


def main_kernel(
    cfg,
    pair_ref, nloc, mask_ref, left_ref, add_ref, wq_ref, wkv_ref, wg_ref, gb_ref, wo_ref,
    out_ref,
    xbuf, rbuf, bias, nall, qn, osend, orecv, lsel, msel, strans, srecv,
    xsem, own_sem, ring_send, ring_recv, q_send, q_recv, o_send, o_recv, s_send, s_recv,
):
    n_row, n_col, rows, cols, cz, heads, rows_dev, selected = cfg
    head_dim = cz // heads
    per = selected // n_col
    half = n_row // 2
    first_half = rows_dev // 2
    MESH = pl.DeviceIdType.MESH
    r = lax.axis_index("row")
    c = lax.axis_index("col")

    def row_of(pos):
        pos = lax.rem(pos + 2 * n_row, n_row)
        return jnp.where(pos < half, 2 * pos, 2 * (n_row - 1 - pos) + 1)

    odd = lax.rem(r, 2)
    pos = jnp.where(odd == 0, r // 2, n_row - 1 - r // 2)
    nexts = (row_of(pos + 1), row_of(pos - 1))
    root = (r * rows) // cols
    start = pl.multiple_of(lax.rem(r * rows, cols), rows)
    is_root = c == root

    def x_copy(k):
        where = pl.ds(k * ROWS_CHUNK, ROWS_CHUNK)
        return pltpu.make_async_copy(pair_ref.at[where], xbuf.at[where], xsem.at[k])

    chunks = rows // ROWS_CHUNK
    for k in range(chunks):
        x_copy(k).start()
    own = pltpu.make_async_copy(nloc, nall.at[pl.ds(r * rows_dev, rows_dev)], own_sem)
    own.start()

    barrier = pltpu.get_barrier_semaphore()
    for nb in nexts:
        pl.semaphore_signal(barrier, inc=1, device_id=(nb, c), device_id_type=MESH)
    for dc in range(1, n_col):
        pl.semaphore_signal(
            barrier, inc=1, device_id=(r, lax.rem(c + dc, n_col)), device_id_type=MESH
        )
    pl.semaphore_wait(barrier, 2 + n_col - 1)

    def valid(way, s, u):
        if s < half:
            return True
        return s == half and ((u < first_half) if way == 0 else (u >= first_half))

    def ring(way, s, u):
        origin = row_of(pos - (s - 1) if way == 0 else pos + (s - 1))
        t = origin * rows_dev + u
        return pltpu.make_async_remote_copy(
            src_ref=nloc.at[u] if s == 1 else nall.at[t],
            dst_ref=nall.at[t],
            send_sem=ring_send.at[way],
            recv_sem=ring_recv.at[way, s - 1, u],
            device_id=(nexts[way], c),
            device_id_type=MESH,
        )

    def q_local(t):
        return pltpu.make_async_copy(nall.at[t, pl.ds(start, rows)], qn.at[t], q_recv.at[t])

    def q_remote(t, dc):
        return pltpu.make_async_remote_copy(
            src_ref=nall.at[t, pl.ds(start, rows)],
            dst_ref=qn.at[t],
            send_sem=q_send.at[dc - 1],
            recv_sem=q_recv.at[t],
            device_id=(r, lax.rem(c + dc, n_col)),
            device_id_type=MESH,
        )

    def q_share(t):
        @pl.when(is_root)
        def _():
            for dc in range(1, n_col):
                q_remote(t, dc).start()
            q_local(t).start()

    for u in range(rows_dev):
        for way in (0, 1):
            ring(way, 1, u).start()
    own.wait()
    for u in range(rows_dev):
        q_share(r * rows_dev + u)

    events = [
        [(way, s, u) for way in (0, 1) if valid(way, s, u)]
        for s in range(1, half + 1)
        for u in range(rows_dev)
    ]

    def arrive(way, s, u):
        t = row_of(pos - s if way == 0 else pos + s) * rows_dev + u
        pltpu.make_async_remote_copy(
            src_ref=nall.at[t],
            dst_ref=nall.at[t],
            send_sem=ring_send.at[way],
            recv_sem=ring_recv.at[way, s - 1, u],
            device_id=(nexts[way], c),
            device_id_type=MESH,
        ).wait_recv()
        if valid(way, s + 1, u):
            ring(way, s + 1, u).start()
        q_share(t)

    row_i = lax.broadcasted_iota(jnp.int32, (cz, cz), 0)
    col_i = lax.broadcasted_iota(jnp.int32, (cz, cz), 1)
    centring = (jnp.where(row_i == col_i, 1.0, 0.0) - 1.0 / cz).astype(BF16)
    left = left_ref[...]

    def bias_step(j0):
        j0 = pl.multiple_of(j0, ROWS_STEP)
        x = xbuf[pl.ds(j0, ROWS_STEP)].reshape(ROWS_STEP * cols, cz)
        d = jnp.dot(x, centring, preferred_element_type=F32).astype(BF16)
        both = jnp.concatenate([d, d * d], axis=-1)
        res = lax.dot_general(
            left, both, (((1,), (1,)), ((), ())), preferred_element_type=F32
        )
        for jj in range(ROWS_STEP):
            at = pl.ds(pl.multiple_of((j0 + jj) * 16, 16), 16)
            for part in range(cols // 128):
                first = jj * cols + part * 128
                rbuf[part, at, :] = res[:, first : first + 128]

    for k in range(chunks):
        x_copy(k).wait()

        def one(b, _, k=k):
            bias_step(k * ROWS_CHUNK + b * ROWS_STEP)
            return 0

        lax.fori_loop(0, ROWS_CHUNK // ROWS_STEP, one, 0)
        lo = k * len(events) // chunks
        hi = (k + 1) * len(events) // chunks
        for group in events[lo:hi]:
            for way, s, u in group:
                arrive(way, s, u)

    for part in range(cols // 128):
        lanes = slice(part * 128, (part + 1) * 128)
        rstd = lax.rsqrt(rbuf[part, pl.ds(2 * heads, rows, stride=16), :] + 1e-05)
        live = mask_ref[:, lanes] > 0
        for h in range(heads):
            raw = (
                rbuf[part, pl.ds(h, rows, stride=16), :]
                + rbuf[part, pl.ds(heads + h, rows, stride=16), :]
            )
            full = raw * rstd + add_ref[h]
            bias[pl.ds(h * rows, rows), lanes] = jnp.where(live, full, F32(-1e9))

    lane = lax.broadcasted_iota(jnp.int32, (rows, cz), 1)
    in_head = [(lane // head_dim) == h for h in range(heads)]
    ones = jnp.ones((cols, cz), BF16)
    lsel[...] = jnp.ones_like(lsel)
    msel[...] = jnp.zeros_like(msel)
    scale = F32(1.0 / (head_dim ** 0.5))

    def o_copy(t, peer):
        return pltpu.make_async_remote_copy(
            src_ref=osend.at[t],
            dst_ref=orecv.at[c, lax.rem(t, per)],
            send_sem=o_send.at[peer],
            recv_sem=o_recv.at[c],
            device_id=(r, peer),
            device_id_type=MESH,
        )

    def attend(t):
        q_local(t).wait()
        kv = jnp.dot(nall[t], wkv_ref[...], preferred_element_type=F32).astype(BF16)
        key = kv[:, :cz]
        value = jnp.concatenate([kv[:, cz:], ones], axis=-1)
        q = (jnp.dot(qn[t], wq_ref[...], preferred_element_type=F32) * scale).astype(BF16)
        q4 = jnp.concatenate([jnp.where(in_head[h], q, jnp.zeros_like(q)) for h in range(heads)], 0)
        s = lax.dot_general(q4, key, (((1,), (1,)), ((), ())), preferred_element_type=F32)
        s = s + bias[...]
        m = jnp.max(s, axis=-1, keepdims=True)
        p = jnp.exp(s - m).astype(BF16)
        o = jnp.dot(p, value, preferred_element_type=F32)
        num = jnp.zeros((rows, cz), F32)
        den = jnp.zeros((rows, cz), F32)
        ls = lsel[...]
        ms = msel[...]
        for h in range(heads):
            oh = o[h * rows : (h + 1) * rows, :cz]
            lh = o[h * rows : (h + 1) * rows, cz:]
            num = jnp.where(in_head[h], oh, num)
            den = jnp.where(in_head[h], lh, den)
            here = lane == t * heads + h
            ls = jnp.where(here, lh, ls)
            ms = jnp.where(here, m[h * rows : (h + 1) * rows], ms)
        lsel[...] = ls
        msel[...] = ms
        osend[t] = (num / den).astype(BF16)

    for dc in range(1, n_col):
        peer = lax.rem(c + dc, n_col)

        def step(i, _, peer=peer):
            t = peer * per + i
            attend(t)
            o_copy(t, peer).start()
            return 0

        lax.fori_loop(0, per, step, 0)

    def step_own(i, _):
        attend(c * per + i)
        return 0

    lax.fori_loop(0, per, step_own, 0)

    strans[...] = jnp.transpose(msel[...] + jnp.log(lsel[...]))
    ph = per * heads

    def s_copy(peer):
        return pltpu.make_async_remote_copy(
            src_ref=strans.at[pl.ds(pl.multiple_of(peer * ph, 8), ph)],
            dst_ref=srecv.at[pl.ds(pl.multiple_of(c * ph, 8), ph)],
            send_sem=s_send.at[peer],
            recv_sem=s_recv.at[c],
            device_id=(r, peer),
            device_id_type=MESH,
        )

    for dc in range(1, n_col):
        s_copy(lax.rem(c + dc, n_col)).start()
    own_rows = pl.ds(pl.multiple_of(c * ph, 8), ph)
    srecv[own_rows, :] = strans[own_rows, :]

    gates = []
    for i in range(per):
        g = jnp.dot(qn[c * per + i], wg_ref[...], preferred_element_type=F32) + gb_ref[...]
        gates.append(jax.nn.sigmoid(g).astype(BF16).astype(F32))
    span = selected * heads
    er = lax.broadcasted_iota(jnp.int32, (span, n_col * per * cz), 0)
    ec = lax.broadcasted_iota(jnp.int32, (span, n_col * per * cz), 1)
    expand = jnp.where(er == ec // head_dim, 1.0, 0.0).astype(BF16)

    for dc in range(1, n_col):
        src = lax.rem(c + dc, n_col)
        pltpu.make_async_remote_copy(
            src_ref=strans.at[pl.ds(0, ph)],
            dst_ref=srecv.at[pl.ds(pl.multiple_of(src * ph, 8), ph)],
            send_sem=s_send.at[src],
            recv_sem=s_recv.at[src],
            device_id=(r, src),
            device_id_type=MESH,
        ).wait_recv()
    stats = [srecv[pl.ds(k * ph, ph), :] for k in range(n_col)]
    top = functools.reduce(jnp.maximum, stats)
    weights = [jnp.exp(a - top) for a in stats]
    total = functools.reduce(jnp.add, weights)
    parts = jnp.concatenate([w / total for w in weights], axis=0)
    spread_w = jnp.dot(jnp.transpose(parts).astype(BF16), expand, preferred_element_type=F32)

    for dc in range(1, n_col):
        src = lax.rem(c + dc, n_col)
        pltpu.make_async_remote_copy(
            src_ref=osend.at[pl.ds(0, per)],
            dst_ref=orecv.at[src],
            send_sem=o_send.at[src],
            recv_sem=o_recv.at[src],
            device_id=(r, src),
            device_id_type=MESH,
        ).wait_recv()
    for i in range(per):
        orecv[c, i] = osend[c * per + i]
    for i in range(per):
        acc = jnp.zeros((rows, cz), F32)
        for k in range(n_col):
            at = (k * per + i) * cz
            acc = acc + spread_w[:, at : at + cz] * orecv[k, i].astype(F32)
        gated = (gates[i] * acc).astype(BF16)
        out_ref[i] = jnp.dot(gated, wo_ref[...], preferred_element_type=F32).astype(BF16)

    for dc in range(1, n_col):
        peer = lax.rem(c + dc, n_col)
        s_copy(peer).wait_send()
        pltpu.make_async_remote_copy(
            src_ref=osend.at[pl.ds(0, per)],
            dst_ref=orecv.at[c],
            send_sem=o_send.at[peer],
            recv_sem=o_recv.at[c],
            device_id=(r, peer),
            device_id_type=MESH,
        ).wait_send()

        @pl.when(is_root)
        def _(dc=dc):
            pltpu.make_async_remote_copy(
                src_ref=qn,
                dst_ref=qn,
                send_sem=q_send.at[dc - 1],
                recv_sem=q_recv.at[0],
                device_id=(r, lax.rem(c + dc, n_col)),
                device_id_type=MESH,
            ).wait_send()

    for way in (0, 1):
        count = sum(valid(way, s, u) for s in range(1, half + 1) for u in range(rows_dev))
        pltpu.make_async_remote_copy(
            src_ref=nall.at[pl.ds(0, count)],
            dst_ref=nall.at[pl.ds(0, count)],
            send_sem=ring_send.at[way],
            recv_sem=ring_recv.at[way, 0, 0],
            device_id=(nexts[way], c),
            device_id_type=MESH,
        ).wait_send()


def body(
    pair_rep, row_ids, pad_mask, ln_gain, ln_bias, w_query, w_key, w_value, w_gate, gate_bias,
    w_bias, w_out,
):
    rows, cols, cz = pair_rep.shape
    heads = w_bias.shape[1]
    n_row = lax.axis_size("row")
    n_col = lax.axis_size("col")
    rows_dev = row_ids.shape[0]
    selected = rows_dev * n_row
    per = selected // n_col
    half = n_row // 2
    offsets = row_ids - lax.axis_index("row") * rows
    nloc = chosen_normed(pair_rep, offsets, ln_gain[None], ln_bias[None])
    scaled = (ln_gain[:, None] * w_bias.astype(F32)).T
    high = scaled.astype(BF16)
    low = (scaled - high.astype(F32)).astype(BF16)
    zero = jnp.zeros_like(high)
    left = jnp.concatenate(
        [
            jnp.concatenate([high, zero], 1),
            jnp.concatenate([low, zero], 1),
            jnp.concatenate([jnp.zeros((1, cz), BF16), jnp.full((1, cz), 1.0 / cz, BF16)], 1),
            jnp.zeros((16 - 2 * heads - 1, 2 * cz), BF16),
        ],
        0,
    )
    add = jnp.sum(ln_bias[:, None] * w_bias.astype(F32), axis=0)
    cfg = (n_row, n_col, rows, cols, cz, heads, rows_dev, selected)
    DMA = pltpu.SemaphoreType.DMA
    return pl.pallas_call(
        functools.partial(main_kernel, cfg),
        out_shape=jax.ShapeDtypeStruct((per, rows, cz), BF16),
        in_specs=[pl.BlockSpec(memory_space=pl.ANY), VM, VM, VM,
                  pl.BlockSpec(memory_space=pltpu.SMEM), VM, VM, VM, VM, VM],
        out_specs=VM,
        scratch_shapes=[
            pltpu.VMEM((rows, cols, cz), BF16),
            pltpu.VMEM((cols // 128, rows * 16, 128), F32),
            pltpu.VMEM((heads * rows, cols), F32),
            pltpu.VMEM((selected, cols, cz), BF16),
            pltpu.VMEM((selected, rows, cz), BF16),
            pltpu.VMEM((selected, rows, cz), BF16),
            pltpu.VMEM((n_col, per, rows, cz), BF16),
            pltpu.VMEM((rows, cz), F32),
            pltpu.VMEM((rows, cz), F32),
            pltpu.VMEM((cz, rows), F32),
            pltpu.VMEM((selected * heads, rows), F32),
            DMA((rows // ROWS_CHUNK,)),
            DMA,
            DMA((2,)),
            DMA((2, half, rows_dev)),
            DMA((n_col - 1,)),
            DMA((selected,)),
            DMA((n_col,)),
            DMA((n_col,)),
            DMA((n_col,)),
            DMA((n_col,)),
        ],
        compiler_params=pltpu.CompilerParams(
            collective_id=0, has_side_effects=True, vmem_limit_bytes=56 * 2**20
        ),
    )(
        pair_rep, nloc, pad_mask[None], left, add, w_query,
        jnp.concatenate([w_key, w_value], axis=1), w_gate, gate_bias[None], w_out,
    )


def solution(mesh):
    return jax.shard_map(
        body,
        mesh=mesh,
        in_specs=(P("row", "col", None), P("row"), P("col")) + (P(),) * 9,
        out_specs=P("col", "row", None),
        check_vma=False,
    )
```

time: 171 us -> 49.6 us (0.29)
  waiting for transfers between devices: 52 us -> 0 us
  Pallas kernels: 0 us -> 41.6 us
  other arithmetic: 46.9 us -> 6.02 us
  matrix products: 29.8 us -> 0 us
  local copies, waits for them, and re-layouts: 17 us -> 1.65 us
  between operations: 13.5 us -> 0.01 us
  blocking collectives: 10.7 us -> 0 us
    pallas_call x0 -> x2, Pallas kernels: none -> 41.6 us  [the longest x1 39 us: body(): pl.pallas_call(functools.partial(main_kernel, cfg), out_shape=jax.ShapeDt...]
    dot_general x14 -> x0, matrix products: 29.8 us -> none  [the longest x1 11.4 us: body(): jnp.einsum('jkc,ch->hjk', normed, w_bias, preferred_element_type=jnp.floa...]
    psum x1 -> x0, waiting for transfers between devices: 26.5 us -> none  [from_root(): return lax.psum(kept, axis)]
    all_gather x2 -> x0, waiting for transfers between devices: 25.4 us -> none  [the longest x1 15.1 us: body(): raw_all = lax.all_gather(raw_chosen, 'row', axis=0, tiled=True)]
    reduce_sum x10 -> x1, other arithmetic: 24.6 us -> 1.35 us  [body(): add = jnp.sum(ln_bias[:, None] * w_bias.astype(F32), axis=0)]
    add x6 -> x0, other arithmetic: 17.6 us -> none  [the longest x3 17.4 us: combine_parts(): summed_a * scale_a[..., None] + summed_b * scale_b[..., None]]
    all_gather x2 -> x0, blocking collectives: 10.7 us -> none  [merged(): lax.all_gather(a.astype(kind), axis)]
    dynamic_slice x10 -> x0, local copies, waits for them, and re-layouts: 6.37 us -> none  [the longest x9 6.36 us: take(): lax.dynamic_index_in_dim(a, source, 0, False).astype(own.dtype)]
  transfers between devices with their start and end apart: 3 -> 0, of which waited for: 3 -> 0; matrix products, arithmetic and copies ran while one was open for 21% -> 0% of each run, Pallas kernels for 0% -> 0%
where the time goes in v1:
time: 49.6 us; the launch traced here: 49.3 us
  Pallas kernels  41.6 us (84%)
  other arithmetic  6.02 us (12%)
  local copies, waits for them, and re-layouts  1.65 us (3%)
    pallas_call x1, Pallas kernels, body(): pl.pallas_call(functools.partial(main_kernel, cfg), out_shape=jax.ShapeDt...  39 us
    pallas_call x1, Pallas kernels, chosen_normed(): pl.pallas_call(norm_kernel, out_shape=jax.ShapeDtypeStruct((offsets.shape...  2.58 us
    unnamed x1, local copies, waits for them, and re-layouts  1.57 us
    concatenate x1, other arithmetic, body(): jnp.concatenate([w_key, w_value], axis=1)  1.4 us
    reduce_sum x1, other arithmetic, body(): add = jnp.sum(ln_bias[:, None] * w_bias.astype(F32), axis=0)  1.35 us
    concatenate x1, other arithmetic, body(): jnp.concatenate([jnp.concatenate([high, zero], 1), jnp.concatenate([low,...  1.34 us
    sub x1, other arithmetic, body(): offsets = row_ids - lax.axis_index('row') * rows  1.25 us

profile of v1, /device:TPU:0, one launch (start us, length us, event | category | flops | bytes accessed | tf_op | source)
XLA Modules:
  0.0 49.3 jit_solution(10253617353481933803)
XLA Ops:
  0.0 1.2 %broadcast_subtract_fusion.ids = s32[2]{0:T(128)} fusion(s32[2]{0:T(128)} %param.13, s32[]{:T(128)S(6)} %mul.19), kind=kLoop, calls=%fused_computation.17 | loop fusion | flops 2 | bytes 20 | tf_op jit(solution)/shard_map/sub | solution.py:370
  1.3 0.1 pad.7.clone
  1.3 0.7 %fusion.9 = bf16[4,128]{1,0:T(4,128)(2,1)S(1)} fusion(bf16[128,4]{0,1:T(4,128)(2,1)} %param.22, f32[128]{0:T(128)} %param.15), kind=kLoop, calls=%fused_computation.15 | loop fusion | flops 3072 | bytes 2560 | tf_op jit(solution)/shard_map/convert_element_type | solution.py:374
  2.0 1.3 %fusion.10 = (f32[4]{0:T(128)}, bf16[4,128]{1,0:T(4,128)(2,1)S(1)}) fusion(bf16[128,4]{0,1:T(4,128)(2,1)} %param.22, f32[128]{0:T(128)} %param.16, f32[128]{0:T(128)} %param.15), kind=kLoop, calls=%fused_computation.16 | loop fusion | flops 2556 | bytes 3088 | tf_op jit(solution)/shard_map/reduce_sum | solution.py:385
  3.4 1.3 %fusion.5.left_ref = bf16[16,256]{1,0:T(8,128)(2,1)} fusion(bf16[4,128]{1,0:T(4,128)(2,1)S(1)} %fusion.9, bf16[4,128]{1,0:T(4,128)(2,1)S(1)} %get-tuple-element.6, bf16[1,256]{1,0:T(2,128)(2,1)} %constant.5.clone.1, bf16[16]{0:T(256)(128)(2,1)S(1)} %pad.7.clone), kind=kLoop, calls=%fused_computation.9 | loop fusion | flops 57344 | bytes 10784 | tf_op jit(solution)/shard_map/concatenate | solution.py:376
  4.7 1.4 %pad_maximum_fusion.wkv_ref = bf16[128,256]{1,0:T(8,128)(2,1)} fusion(bf16[128,128]{1,0:T(8,128)(2,1)} %param.19, bf16[128,128]{1,0:T(8,128)(2,1)} %param.18), kind=kLoop, calls=%fused_computation | loop fusion | flops 131072 | bytes 131072 | tf_op jit(solution)/shard_map/concatenate | solution.py:422
  6.1 2.6 %shard_map.118.nloc = bf16[2,256,128]{2,1,0:T(8,128)(2,1)} custom-call(s32[2]{0:T(128)} %broadcast_subtract_fusion.ids, bf16[128,256,128]{2,1,0:T(8,128)(2,1)} %pair_ref.1, f32[1,128]{1,0:T(1,128)} %bitcast.14, f32[1,128]{1,0:T(1,128)} %bitcast.15), custom_call_target="tpu_custom_call" | custom-call | tf_op jit(solution)/shard_map/pallas_call | solution.py:26
  8.7 39.0 %shard_map.119 = bf16[4,128,128]{2,1,0:T(8,128)(2,1)} custom-call(bf16[128,256,128]{2,1,0:T(8,128)(2,1)} %pair_ref.1, bf16[2,256,128]{2,1,0:T(8,128)(2,1)} %shard_map.118.nloc, s32[1,256]{1,0:T(1,128)} %bitcast.16, bf16[16,256]{1,0:T(8,128)(2,1)} %fusion.5.left_ref, f32[4]{0:T(128)} %get-tuple-element.5.add_ref, bf16[128,128]{1,0:T(8,128)(2,1)} %wq_ref.1, ...), custom_call_target="tpu_custom_call" | custom-call | tf_op jit(solution)/shard_map/pallas_call | solution.py:388
  47.7 1.6 %copy.14 = bf16[4,128,128]{2,1,0:T(8,128)(2,1)} copy(bf16[4,128,128]{2,1,0:T(8,128)(2,1)} %shard_map.119) | data formatting | bytes 262144
  (1 shorter events, 0.0 us)

commit v2 on v1

--- a/solution.py
+++ b/solution.py
@@ -30,7 +30,7 @@
             num_scalar_prefetch=1,
             grid=(offsets.shape[0],),
             in_specs=[
-                pl.BlockSpec((1, cols, cz), lambda i, ids: (ids[i], 0, 0)),
+                pl.BlockSpec((1, cols, cz), lambda i, ids: (lax.rem(ids[i], rows), 0, 0)),
                 pl.BlockSpec((1, cz), lambda i, ids: (0, 0)),
                 pl.BlockSpec((1, cz), lambda i, ids: (0, 0)),
             ],
@@ -41,7 +41,8 @@
 
 def main_kernel(
     cfg,
-    pair_ref, nloc, mask_ref, left_ref, add_ref, wq_ref, wkv_ref, wg_ref, gb_ref, wo_ref,
+    pair_ref, nloc, mask_ref, gain_ref, shift_ref, wb_ref, wq_ref, wk_ref, wv_ref, wg_ref, gb_ref,
+    wo_ref,
     out_ref,
     xbuf, rbuf, bias, nall, qn, osend, orecv, lsel, msel, strans, srecv,
     xsem, own_sem, ring_send, ring_recv, q_send, q_recv, o_send, o_recv, s_send, s_recv,
@@ -152,7 +153,23 @@
     row_i = lax.broadcasted_iota(jnp.int32, (cz, cz), 0)
     col_i = lax.broadcasted_iota(jnp.int32, (cz, cz), 1)
     centring = (jnp.where(row_i == col_i, 1.0, 0.0) - 1.0 / cz).astype(BF16)
-    left = left_ref[...]
+    pick = lax.broadcasted_iota(jnp.int32, (16, heads), 0)
+    head_i = lax.broadcasted_iota(jnp.int32, (16, heads), 1)
+    pick = jnp.where((pick == head_i) | (pick == head_i + heads), 1.0, 0.0).astype(BF16)
+    by_head = lax.dot_general(
+        pick, wb_ref[...], (((1,), (0,)), ((), ())), preferred_element_type=F32
+    )
+    add = jnp.sum(by_head * shift_ref[...], axis=-1, keepdims=True)
+    scaled = by_head * gain_ref[...]
+    high = scaled.astype(BF16).astype(F32)
+    line = lax.broadcasted_iota(jnp.int32, (16, cz), 0)
+    left = jnp.concatenate(
+        [
+            jnp.where(line < heads, high, scaled - high),
+            jnp.where(line == 2 * heads, F32(1.0 / cz), F32(0.0)),
+        ],
+        axis=-1,
+    ).astype(BF16)
 
     def bias_step(j0):
         j0 = pl.multiple_of(j0, ROWS_STEP)
@@ -191,12 +208,13 @@
                 rbuf[part, pl.ds(h, rows, stride=16), :]
                 + rbuf[part, pl.ds(heads + h, rows, stride=16), :]
             )
-            full = raw * rstd + add_ref[h]
+            full = raw * rstd + add[h : h + 1]
             bias[pl.ds(h * rows, rows), lanes] = jnp.where(live, full, F32(-1e9))
 
     lane = lax.broadcasted_iota(jnp.int32, (rows, cz), 1)
     in_head = [(lane // head_dim) == h for h in range(heads)]
     ones = jnp.ones((cols, cz), BF16)
+    wkv = jnp.concatenate([wk_ref[...], wv_ref[...]], axis=-1)
     lsel[...] = jnp.ones_like(lsel)
     msel[...] = jnp.zeros_like(msel)
     scale = F32(1.0 / (head_dim ** 0.5))
@@ -213,7 +231,7 @@
 
     def attend(t):
         q_local(t).wait()
-        kv = jnp.dot(nall[t], wkv_ref[...], preferred_element_type=F32).astype(BF16)
+        kv = jnp.dot(nall[t], wkv, preferred_element_type=F32).astype(BF16)
         key = kv[:, :cz]
         value = jnp.concatenate([kv[:, cz:], ones], axis=-1)
         q = (jnp.dot(qn[t], wq_ref[...], preferred_element_type=F32) * scale).astype(BF16)
@@ -367,29 +385,13 @@
     selected = rows_dev * n_row
     per = selected // n_col
     half = n_row // 2
-    offsets = row_ids - lax.axis_index("row") * rows
-    nloc = chosen_normed(pair_rep, offsets, ln_gain[None], ln_bias[None])
-    scaled = (ln_gain[:, None] * w_bias.astype(F32)).T
-    high = scaled.astype(BF16)
-    low = (scaled - high.astype(F32)).astype(BF16)
-    zero = jnp.zeros_like(high)
-    left = jnp.concatenate(
-        [
-            jnp.concatenate([high, zero], 1),
-            jnp.concatenate([low, zero], 1),
-            jnp.concatenate([jnp.zeros((1, cz), BF16), jnp.full((1, cz), 1.0 / cz, BF16)], 1),
-            jnp.zeros((16 - 2 * heads - 1, 2 * cz), BF16),
-        ],
-        0,
-    )
-    add = jnp.sum(ln_bias[:, None] * w_bias.astype(F32), axis=0)
+    nloc = chosen_normed(pair_rep, row_ids, ln_gain[None], ln_bias[None])
     cfg = (n_row, n_col, rows, cols, cz, heads, rows_dev, selected)
     DMA = pltpu.SemaphoreType.DMA
     return pl.pallas_call(
         functools.partial(main_kernel, cfg),
         out_shape=jax.ShapeDtypeStruct((per, rows, cz), BF16),
-        in_specs=[pl.BlockSpec(memory_space=pl.ANY), VM, VM, VM,
-                  pl.BlockSpec(memory_space=pltpu.SMEM), VM, VM, VM, VM, VM],
+        in_specs=[pl.BlockSpec(memory_space=pl.ANY)] + [VM] * 11,
         out_specs=VM,
         scratch_shapes=[
             pltpu.VMEM((rows, cols, cz), BF16),
@@ -418,8 +420,8 @@
             collective_id=0, has_side_effects=True, vmem_limit_bytes=56 * 2**20
         ),
     )(
-        pair_rep, nloc, pad_mask[None], left, add, w_query,
-        jnp.concatenate([w_key, w_value], axis=1), w_gate, gate_bias[None], w_out,
+        pair_rep, nloc, pad_mask[None], ln_gain[None], ln_bias[None], w_bias.T, w_query, w_key,
+        w_value, w_gate, gate_bias[None], w_out,
     )
 
 

time: 49.6 us -> 43.4 us (0.88)
  other arithmetic: 6.02 us -> 0 us
    concatenate x2 -> x0, other arithmetic: 2.74 us -> none  [the longest x1 1.4 us: body(): jnp.concatenate([w_key, w_value], axis=1)]
    reduce_sum x1 -> x0, other arithmetic: 1.35 us -> none  [body(): add = jnp.sum(ln_bias[:, None] * w_bias.astype(F32), axis=0)]
    sub x1 -> x0, other arithmetic: 1.25 us -> none  [body(): offsets = row_ids - lax.axis_index('row') * rows]
    convert_element_type x1 -> x0, other arithmetic: 0.69 us -> none  [body(): low = (scaled - high.astype(F32)).astype(BF16)]
where the time goes in v2:
time: 43.4 us; the launch traced here: 43.2 us
  Pallas kernels  41.6 us (96%)
  local copies, waits for them, and re-layouts  1.57 us (4%)
    pallas_call x1, Pallas kernels, body(): pl.pallas_call(functools.partial(main_kernel, cfg), out_shape=jax.ShapeDt...  39 us
    pallas_call x1, Pallas kernels, chosen_normed(): pl.pallas_call(norm_kernel, out_shape=jax.ShapeDtypeStruct((offsets.shape...  2.59 us
    unnamed x1, local copies, waits for them, and re-layouts  1.57 us

profile of v2, /device:TPU:0, one launch (start us, length us, event | category | flops | bytes accessed | tf_op | source)
XLA Modules:
  0.0 43.2 jit_solution(5499239560126427588)
XLA Ops:
  0.0 2.6 %shard_map.118.nloc = bf16[2,256,128]{2,1,0:T(8,128)(2,1)} custom-call(s32[2]{0:T(128)} %ids.1, bf16[128,256,128]{2,1,0:T(8,128)(2,1)} %pair_ref.1, f32[1,128]{1,0:T(1,128)} %bitcast.5, f32[1,128]{1,0:T(1,128)} %bitcast.7), custom_call_target="tpu_custom_call" | custom-call | tf_op jit(solution)/shard_map/pallas_call | solution.py:26
  2.6 39.0 %shard_map.119 = bf16[4,128,128]{2,1,0:T(8,128)(2,1)} custom-call(bf16[128,256,128]{2,1,0:T(8,128)(2,1)} %pair_ref.1, bf16[2,256,128]{2,1,0:T(8,128)(2,1)} %shard_map.118.nloc, s32[1,256]{1,0:T(1,128)} %bitcast.9, f32[1,128]{1,0:T(1,128)} %bitcast.6, f32[1,128]{1,0:T(1,128)} %bitcast.8, bf16[4,128]{1,0:T(4,128)(2,1)} %bitcast.10, bf16[128,128]{1,0:T(8,128)(2,1)} %wq_ref.1, ...), custom_call_target="tpu_custom_call" | custom-call | tf_op jit(solution)/shard_map/pallas_call | solution.py:391
  41.6 1.6 %copy.14 = bf16[4,128,128]{2,1,0:T(8,128)(2,1)} copy(bf16[4,128,128]{2,1,0:T(8,128)(2,1)} %shard_map.119) | data formatting | bytes 262144

commit v3 on v2

--- a/solution.py
+++ b/solution.py
@@ -10,7 +10,8 @@
 BF16 = jnp.bfloat16
 VM = pl.BlockSpec(memory_space=pltpu.VMEM)
 ROWS_CHUNK = 16
-ROWS_STEP = 8
+ROWS_STEP = 16
+PIECES = 1
 
 
 def norm_kernel(ids, x_ref, gain_ref, shift_ref, o_ref):
@@ -91,14 +92,17 @@
             return True
         return s == half and ((u < first_half) if way == 0 else (u >= first_half))
 
-    def ring(way, s, u):
+    piece = cols // PIECES
+
+    def ring(way, s, u, b):
         origin = row_of(pos - (s - 1) if way == 0 else pos + (s - 1))
         t = origin * rows_dev + u
+        part = pl.ds(b * piece, piece)
         return pltpu.make_async_remote_copy(
-            src_ref=nloc.at[u] if s == 1 else nall.at[t],
-            dst_ref=nall.at[t],
+            src_ref=nloc.at[u, part] if s == 1 else nall.at[t, part],
+            dst_ref=nall.at[t, part],
             send_sem=ring_send.at[way],
-            recv_sem=ring_recv.at[way, s - 1, u],
+            recv_sem=ring_recv.at[way, s - 1, u, b],
             device_id=(nexts[way], c),
             device_id_type=MESH,
         )
@@ -124,8 +128,9 @@
             q_local(t).start()
 
     for u in range(rows_dev):
-        for way in (0, 1):
-            ring(way, 1, u).start()
+        for b in range(PIECES):
+            for way in (0, 1):
+                ring(way, 1, u, b).start()
     own.wait()
     for u in range(rows_dev):
         q_share(r * rows_dev + u)
@@ -136,19 +141,25 @@
         for u in range(rows_dev)
     ]
 
-    def arrive(way, s, u):
-        t = row_of(pos - s if way == 0 else pos + s) * rows_dev + u
-        pltpu.make_async_remote_copy(
-            src_ref=nall.at[t],
-            dst_ref=nall.at[t],
-            send_sem=ring_send.at[way],
-            recv_sem=ring_recv.at[way, s - 1, u],
-            device_id=(nexts[way], c),
-            device_id_type=MESH,
-        ).wait_recv()
-        if valid(way, s + 1, u):
-            ring(way, s + 1, u).start()
-        q_share(t)
+    def token_row(way, s, u):
+        return row_of(pos - s if way == 0 else pos + s) * rows_dev + u
+
+    def arrive(group):
+        for b in range(PIECES):
+            for way, s, u in group:
+                part = nall.at[token_row(way, s, u), pl.ds(b * piece, piece)]
+                pltpu.make_async_remote_copy(
+                    src_ref=part,
+                    dst_ref=part,
+                    send_sem=ring_send.at[way],
+                    recv_sem=ring_recv.at[way, s - 1, u, b],
+                    device_id=(nexts[way], c),
+                    device_id_type=MESH,
+                ).wait_recv()
+                if valid(way, s + 1, u):
+                    ring(way, s + 1, u, b).start()
+        for way, s, u in group:
+            q_share(token_row(way, s, u))
 
     row_i = lax.broadcasted_iota(jnp.int32, (cz, cz), 0)
     col_i = lax.broadcasted_iota(jnp.int32, (cz, cz), 1)
@@ -193,11 +204,10 @@
             return 0
 
         lax.fori_loop(0, ROWS_CHUNK // ROWS_STEP, one, 0)
-        lo = k * len(events) // chunks
-        hi = (k + 1) * len(events) // chunks
-        for group in events[lo:hi]:
-            for way, s, u in group:
-                arrive(way, s, u)
+        if k == chunks // 2 - 1:
+            arrive(events[0])
+        if k == chunks * 3 // 4 - 1:
+            arrive(events[1])
 
     for part in range(cols // 128):
         lanes = slice(part * 128, (part + 1) * 128)
@@ -229,8 +239,7 @@
             device_id_type=MESH,
         )
 
-    def attend(t):
-        q_local(t).wait()
+    def attend(t, ls, ms):
         kv = jnp.dot(nall[t], wkv, preferred_element_type=F32).astype(BF16)
         key = kv[:, :cz]
         value = jnp.concatenate([kv[:, cz:], ones], axis=-1)
@@ -243,8 +252,6 @@
         o = jnp.dot(p, value, preferred_element_type=F32)
         num = jnp.zeros((rows, cz), F32)
         den = jnp.zeros((rows, cz), F32)
-        ls = lsel[...]
-        ms = msel[...]
         for h in range(heads):
             oh = o[h * rows : (h + 1) * rows, :cz]
             lh = o[h * rows : (h + 1) * rows, cz:]
@@ -253,26 +260,38 @@
             here = lane == t * heads + h
             ls = jnp.where(here, lh, ls)
             ms = jnp.where(here, m[h * rows : (h + 1) * rows], ms)
+        osend[t] = (num / den).astype(BF16)
+        return ls, ms
+
+    def attend_group(rows_of):
+        for t in rows_of:
+            q_local(t).wait()
+        ls = lsel[...]
+        ms = msel[...]
+        for t in rows_of:
+            ls, ms = attend(t, ls, ms)
         lsel[...] = ls
         msel[...] = ms
-        osend[t] = (num / den).astype(BF16)
-
-    for dc in range(1, n_col):
-        peer = lax.rem(c + dc, n_col)
-
-        def step(i, _, peer=peer):
-            t = peer * per + i
-            attend(t)
-            o_copy(t, peer).start()
-            return 0
-
-        lax.fori_loop(0, per, step, 0)
-
-    def step_own(i, _):
-        attend(c * per + i)
-        return 0
-
-    lax.fori_loop(0, per, step_own, 0)
+        for t in rows_of:
+            peer = t // per
+
+            @pl.when(peer != c)
+            def _(t=t, peer=peer):
+                o_copy(t, peer).start()
+
+    todo = [[r * rows_dev + u for u in range(rows_dev)]]
+    todo += [[token_row(*e) for e in group] for group in events]
+    done = 0
+    for g in range(2, len(events)):
+        arrive(events[g])
+        upto = g - 1 if g < len(events) - 2 else g
+        if g == len(events) - 1:
+            upto = len(todo)
+        if g == len(events) - 1:
+            todo[-2:] = [todo[-2] + todo[-1]]
+        for rows_of in todo[done:upto]:
+            attend_group(rows_of)
+        done = upto
 
     strans[...] = jnp.transpose(msel[...] + jnp.log(lsel[...]))
     ph = per * heads
@@ -367,7 +386,7 @@
             src_ref=nall.at[pl.ds(0, count)],
             dst_ref=nall.at[pl.ds(0, count)],
             send_sem=ring_send.at[way],
-            recv_sem=ring_recv.at[way, 0, 0],
+            recv_sem=ring_recv.at[way, 0, 0, 0],
             device_id=(nexts[way], c),
             device_id_type=MESH,
         ).wait_send()
@@ -408,7 +427,7 @@
             DMA((rows // ROWS_CHUNK,)),
             DMA,
             DMA((2,)),
-            DMA((2, half, rows_dev)),
+            DMA((2, half, rows_dev, PIECES)),
             DMA((n_col - 1,)),
             DMA((selected,)),
             DMA((n_col,)),

time: 43.4 us -> 37.2 us (0.86)
  Pallas kernels: 41.6 us -> 35.4 us
    pallas_call x1, Pallas kernels: 39 us -> 32.8 us  [body(): pl.pallas_call(functools.partial(main_kernel, cfg), out_shape=jax.ShapeDt...]
where the time goes in v3:
time: 37.2 us; the launch traced here: 37 us
  Pallas kernels  35.4 us (95%)
  local copies, waits for them, and re-layouts  1.57 us (4%)
    pallas_call x1, Pallas kernels, body(): pl.pallas_call(functools.partial(main_kernel, cfg), out_shape=jax.ShapeDt...  32.8 us
    pallas_call x1, Pallas kernels, chosen_normed(): pl.pallas_call(norm_kernel, out_shape=jax.ShapeDtypeStruct((offsets.shape...  2.59 us
    unnamed x1, local copies, waits for them, and re-layouts  1.57 us

profile of v3, /device:TPU:0, one launch (start us, length us, event | category | flops | bytes accessed | tf_op | source)
XLA Modules:
  0.0 37.0 jit_solution(13978005001604031835)
XLA Ops:
  0.0 2.6 %shard_map.118.nloc = bf16[2,256,128]{2,1,0:T(8,128)(2,1)} custom-call(s32[2]{0:T(128)} %ids.1, bf16[128,256,128]{2,1,0:T(8,128)(2,1)} %pair_ref.1, f32[1,128]{1,0:T(1,128)} %bitcast.5, f32[1,128]{1,0:T(1,128)} %bitcast.7), custom_call_target="tpu_custom_call" | custom-call | tf_op jit(solution)/shard_map/pallas_call | solution.py:27
  2.6 32.8 %shard_map.119 = bf16[4,128,128]{2,1,0:T(8,128)(2,1)} custom-call(bf16[128,256,128]{2,1,0:T(8,128)(2,1)} %pair_ref.1, bf16[2,256,128]{2,1,0:T(8,128)(2,1)} %shard_map.118.nloc, s32[1,256]{1,0:T(1,128)} %bitcast.9, f32[1,128]{1,0:T(1,128)} %bitcast.6, f32[1,128]{1,0:T(1,128)} %bitcast.8, bf16[4,128]{1,0:T(4,128)(2,1)} %bitcast.10, bf16[128,128]{1,0:T(8,128)(2,1)} %wq_ref.1, ...), custom_call_target="tpu_custom_call" | custom-call | tf_op jit(solution)/shard_map/pallas_call | solution.py:410
  35.4 1.6 %copy.14 = bf16[4,128,128]{2,1,0:T(8,128)(2,1)} copy(bf16[4,128,128]{2,1,0:T(8,128)(2,1)} %shard_map.119) | data formatting | bytes 262144
